TPU v7x, 32 devices: a whole 2x2x4 slice. The times are simulated.
32 devices in a mesh: dp: 2 (over y), head: 16 (over z, x, core).
Axes of the slice: x: 2, y: 2, z: 4, core: 2. Of those that a mesh axis runs over, the one named last changes fastest.
Arguments:
- head_ids: int32 [2, 2048, 8], P('dp', 'head'), may hold values from 0 to 63, as said below
- query_slots: bfloat16 [2, 2048, 8, 128], P('dp', 'head'), may hold values from -300 to 300
- key_slots: bfloat16 [2, 2048, 8, 128], P('dp', 'head'), may hold values from -13 to 13
- value_slots: bfloat16 [2, 2048, 8, 128], P('dp', 'head'), may hold values from -5 to 5
- gate_logits: float32 [2, 2048, 8], P('dp', 'head'), may hold values from -8 to 310
- sink_logits: float32 [64], P('head'), may hold values from 1 to 6
- out_grad: bfloat16 [2, 2048, 8, 128], P('dp', 'head'), may hold values from -6 to 6
Outputs:
- mixed: bfloat16 [2, 2048, 8, 128], P('dp', 'head')
- query_grad: bfloat16 [2, 2048, 8, 128], P('dp', 'head')
- key_grad: bfloat16 [2, 2048, 8, 128], P('dp', 'head')
- value_grad: bfloat16 [2, 2048, 8, 128], P('dp', 'head')
- gate_grad: float32 [2, 2048, 8], P('dp', 'head')
- sink_grad: float32 [64], P('head')
Inputs may be any that keep to these rules, and one draw needn't show every extreme that they name: `head_ids`: each token names 8 different heads. Among the 128 tokens of one device no head is named more than 32 times, and in every group one head is named exactly 32 times by the tokens of every device of that group.
All inputs are finite; a program needn't handle non-finite values.
Results may differ from a plain program's by a relative error of at most 0.023.
Values may be sent and summed in bfloat16 or wider, within the bound.
No kernel may reach another device: no remote copies, remote signals or barrier semaphores. Data moves between devices by JAX's collectives and lax.ppermute only.
A program may use at most 64 MiB of HBM per device.

v0:
```python
import math
import jax
import jax.numpy as jnp
from jax import lax
from jax.sharding import PartitionSpec as P

HEADS = 64
BLOCK = 512
SLOT = 32
masked_value = -1e30


def block_scores(query_tile, key_tile, query_live, key_live, query_offset, key_offset, scale):
    scores = scale * jnp.einsum(
        "qd,kd->qk", query_tile, key_tile, preferred_element_type=jnp.float32
    )
    query_index = query_offset + lax.iota(jnp.int32, query_tile.shape[0])
    key_index = key_offset + lax.iota(jnp.int32, key_tile.shape[0])
    allowed = query_live[:, None] & key_live[None, :] & (key_index[None, :] <= query_index[:, None])
    return (scores, allowed)


def forward_head(query_rows, key_rows, value_rows, live_rows, sink_value, used_blocks, width):
    row_count, head_width = query_rows.shape
    scale = 1.0 / math.sqrt(head_width)

    def forward_query_block(qblock, carry):
        lse_all, out_all = carry
        offset = qblock * width
        query_tile = lax.dynamic_slice_in_dim(query_rows, offset, width, 0)
        query_live = lax.dynamic_slice_in_dim(live_rows, offset, width, 0)

        def tile_at(kblock):
            key_offset = kblock * width
            key_tile = lax.dynamic_slice_in_dim(key_rows, key_offset, width, 0)
            value_tile = lax.dynamic_slice_in_dim(value_rows, key_offset, width, 0)
            key_live = lax.dynamic_slice_in_dim(live_rows, key_offset, width, 0)
            scores, allowed = block_scores(
                query_tile, key_tile, query_live, key_live, offset, key_offset, scale
            )
            return (scores, allowed, value_tile)

        def stat_step(kblock, state):
            run_max, run_sum = state
            scores, allowed, value_tile = tile_at(kblock)
            masked = jnp.where(allowed, scores, masked_value)
            new_max = jnp.maximum(run_max, jnp.max(masked, axis=1))
            new_sum = run_sum * jnp.exp(run_max - new_max) + jnp.sum(
                jnp.where(allowed, jnp.exp(masked - new_max[:, None]), 0.0), axis=1
            )
            return (new_max, new_sum)

        start_state = (jnp.full((width,), sink_value, jnp.float32), jnp.ones((width,), jnp.float32))
        run_max, run_sum = lax.fori_loop(0, qblock + 1, stat_step, start_state)
        row_lse = run_max + jnp.log(run_sum)

        def value_step(kblock, total):
            scores, allowed, value_tile = tile_at(kblock)
            weights = jnp.where(allowed, jnp.exp(scores - row_lse[:, None]), 0.0).astype(
                jnp.bfloat16
            )
            return total + jnp.dot(weights, value_tile, preferred_element_type=jnp.float32)

        total = lax.fori_loop(
            0, qblock + 1, value_step, jnp.zeros((width, head_width), jnp.float32)
        )
        lse_all = lax.dynamic_update_slice_in_dim(lse_all, row_lse, offset, 0)
        out_all = lax.dynamic_update_slice_in_dim(out_all, total.astype(jnp.bfloat16), offset, 0)
        return (lse_all, out_all)

    start_all = (
        jnp.zeros((row_count,), jnp.float32),
        jnp.zeros((row_count, head_width), jnp.bfloat16),
    )
    return lax.fori_loop(0, used_blocks, forward_query_block, start_all)


def backward_head(
    query_rows,
    key_rows,
    value_rows,
    cot_rows,
    head_out,
    lse_all,
    live_rows,
    sink_value,
    used_blocks,
    width,
):
    row_count, head_width = query_rows.shape
    scale = 1.0 / math.sqrt(head_width)
    deltas = jnp.sum(cot_rows.astype(jnp.float32) * head_out.astype(jnp.float32), axis=1)
    sink_term = -jnp.sum(jnp.exp(sink_value - lse_all) * deltas)

    def backward_query_block(qblock, carry):
        qgrad_all, kgrad_acc, vgrad_acc = carry
        offset = qblock * width
        query_tile = lax.dynamic_slice_in_dim(query_rows, offset, width, 0)
        cot_tile = lax.dynamic_slice_in_dim(cot_rows, offset, width, 0)
        lse_tile = lax.dynamic_slice_in_dim(lse_all, offset, width, 0)
        delta_tile = lax.dynamic_slice_in_dim(deltas, offset, width, 0)
        query_live = lax.dynamic_slice_in_dim(live_rows, offset, width, 0)

        def key_step(kblock, inner):
            qgrad_run, kgrad_acc, vgrad_acc = inner
            key_offset = kblock * width
            key_tile = lax.dynamic_slice_in_dim(key_rows, key_offset, width, 0)
            value_tile = lax.dynamic_slice_in_dim(value_rows, key_offset, width, 0)
            key_live = lax.dynamic_slice_in_dim(live_rows, key_offset, width, 0)
            scores, allowed = block_scores(
                query_tile, key_tile, query_live, key_live, offset, key_offset, scale
            )
            probability = jnp.where(allowed, jnp.exp(scores - lse_tile[:, None]), 0.0)
            weights = probability.astype(jnp.bfloat16)
            dprob = jnp.einsum(
                "qd,kd->qk", cot_tile, value_tile, preferred_element_type=jnp.float32
            )
            dscore = (probability * (dprob - delta_tile[:, None])).astype(jnp.bfloat16)
            qgrad_run = qgrad_run + jnp.dot(dscore, key_tile, preferred_element_type=jnp.float32)
            kgrad_part = jnp.einsum(
                "qk,qd->kd", dscore, query_tile, preferred_element_type=jnp.float32
            )
            vgrad_part = jnp.einsum(
                "qk,qd->kd", weights, cot_tile, preferred_element_type=jnp.float32
            )
            kgrad_acc = lax.dynamic_update_slice_in_dim(
                kgrad_acc,
                lax.dynamic_slice_in_dim(kgrad_acc, key_offset, width, 0) + kgrad_part,
                key_offset,
                0,
            )
            vgrad_acc = lax.dynamic_update_slice_in_dim(
                vgrad_acc,
                lax.dynamic_slice_in_dim(vgrad_acc, key_offset, width, 0) + vgrad_part,
                key_offset,
                0,
            )
            return (qgrad_run, kgrad_acc, vgrad_acc)

        start_inner = (jnp.zeros((width, head_width), jnp.float32), kgrad_acc, vgrad_acc)
        qgrad_run, kgrad_acc, vgrad_acc = lax.fori_loop(0, qblock + 1, key_step, start_inner)
        qgrad_all = lax.dynamic_update_slice_in_dim(
            qgrad_all, (scale * qgrad_run).astype(jnp.bfloat16), offset, 0
        )
        return (qgrad_all, kgrad_acc, vgrad_acc)

    start_all = (
        jnp.zeros((row_count, head_width), jnp.bfloat16),
        jnp.zeros((row_count, head_width), jnp.float32),
        jnp.zeros((row_count, head_width), jnp.float32),
    )
    qgrad_all, kgrad_acc, vgrad_acc = lax.fori_loop(0, used_blocks, backward_query_block, start_all)
    return (
        qgrad_all,
        (scale * kgrad_acc).astype(jnp.bfloat16),
        vgrad_acc.astype(jnp.bfloat16),
        sink_term,
    )


def arrange(live_rows, width):
    row_count = live_rows.shape[0]
    return (None, None, row_count // width)


def pick_rows(buffer, head_slot):
    picked = buffer[:, head_slot].reshape(-1, buffer.shape[-1])
    return picked


def restore(row_block, devices):
    return row_block.reshape(devices, -1, row_block.shape[-1])


def per_device(head_ids, query_slots, key_slots, value_slots, gate_logits, sink_logits, out_grad):
    devices = lax.axis_size("head")
    local_heads = HEADS // devices
    selected = head_ids[0]
    token_count, slot_count = selected.shape
    head_width = query_slots.shape[-1]
    matches = (selected[:, :, None] == lax.iota(jnp.int32, HEADS)[None, None, :]).astype(jnp.int32)
    per_token = jnp.sum(matches, axis=1)
    earlier = jnp.cumsum(per_token, axis=0) - per_token
    placing = jnp.sum(matches * earlier[:, None, :], axis=2)
    target = (selected * SLOT + placing).reshape(-1)
    buffer_rows = HEADS * SLOT

    def spread_out(flat_rows):
        filled_rows = (
            jnp.zeros((buffer_rows, flat_rows.shape[-1]), flat_rows.dtype).at[target].set(flat_rows)
        )
        return filled_rows.reshape(devices, local_heads, SLOT, flat_rows.shape[-1])

    def collect(buffer):
        return buffer.reshape(buffer_rows, buffer.shape[-1])[target].reshape(
            token_count, slot_count, buffer.shape[-1]
        )

    gate_probs = jax.nn.softmax(gate_logits[0], axis=-1)
    cotangent = (gate_probs[:, :, None] * out_grad[0].astype(jnp.float32)).astype(jnp.bfloat16)
    send_query = spread_out(query_slots[0].reshape(-1, head_width))
    send_key = spread_out(key_slots[0].reshape(-1, head_width))
    send_value = spread_out(value_slots[0].reshape(-1, head_width))
    send_cot = spread_out(cotangent.reshape(-1, head_width))
    filled = (
        jnp.zeros((buffer_rows,), jnp.bfloat16)
        .at[target]
        .set(jnp.ones((), jnp.bfloat16))
        .reshape(devices, local_heads, SLOT)
    )
    out_list, qgrad_list, kgrad_list, vgrad_list, sink_list = ([], [], [], [], [])
    recv_query, recv_key, recv_value, recv_fill = (
        lax.all_to_all(send_query, "head", split_axis=0, concat_axis=0, tiled=True),
        lax.all_to_all(send_key, "head", split_axis=0, concat_axis=0, tiled=True),
        lax.all_to_all(send_value, "head", split_axis=0, concat_axis=0, tiled=True),
        lax.all_to_all(filled, "head", split_axis=0, concat_axis=0, tiled=True),
    )
    prepared = []
    lse_list = []
    head_outs = []
    for head_slot in range(local_heads):
        live_rows = recv_fill[:, head_slot].reshape(-1) > 0
        gather_order, landing, used_blocks = arrange(live_rows, BLOCK)
        live_use = live_rows
        pieces = (
            pick_rows(recv_query, head_slot),
            pick_rows(recv_key, head_slot),
            pick_rows(recv_value, head_slot),
        )
        pieces, live_use, gather_order, landing, used_blocks = (
            pieces,
            live_use,
            gather_order,
            landing,
            used_blocks,
        )
        row_lse, head_out = forward_head(
            pieces[0], pieces[1], pieces[2], live_use, sink_logits[head_slot], used_blocks, BLOCK
        )
        prepared.append((pieces, live_use, gather_order, landing, used_blocks))
        lse_list.append(row_lse)
        head_outs.append(head_out)
        out_list.append(restore(head_out, devices))
    back_out = lax.all_to_all(
        jnp.stack(out_list, axis=1), "head", split_axis=0, concat_axis=0, tiled=True
    )
    recv_cot = lax.all_to_all(send_cot, "head", split_axis=0, concat_axis=0, tiled=True)
    for head_slot in range(local_heads):
        pieces, live_use, gather_order, landing, used_blocks = prepared[head_slot]
        cot_rows = pick_rows(recv_cot, head_slot)
        qgrad, kgrad, vgrad, sink_term = backward_head(
            pieces[0],
            pieces[1],
            pieces[2],
            cot_rows,
            head_outs[head_slot],
            lse_list[head_slot],
            live_use,
            sink_logits[head_slot],
            used_blocks,
            BLOCK,
        )
        qgrad_list.append(restore(qgrad, devices))
        kgrad_list.append(restore(kgrad, devices))
        vgrad_list.append(restore(vgrad, devices))
        sink_list.append(sink_term)
    back_qgrad, back_kgrad, back_vgrad = (
        lax.all_to_all(
            jnp.stack(qgrad_list, axis=1), "head", split_axis=0, concat_axis=0, tiled=True
        ),
        lax.all_to_all(
            jnp.stack(kgrad_list, axis=1), "head", split_axis=0, concat_axis=0, tiled=True
        ),
        lax.all_to_all(
            jnp.stack(vgrad_list, axis=1), "head", split_axis=0, concat_axis=0, tiled=True
        ),
    )
    sink_grad = lax.psum(jnp.stack(sink_list), "dp")
    token_out = collect(back_out).astype(jnp.float32)
    mixed = (gate_probs[:, :, None] * token_out).astype(jnp.bfloat16)
    gate_sum = jnp.sum(out_grad[0].astype(jnp.float32) * token_out, axis=-1)
    gate_grad = gate_probs * (gate_sum - jnp.sum(gate_probs * gate_sum, axis=-1, keepdims=True))
    return (
        mixed[None],
        collect(back_qgrad)[None],
        collect(back_kgrad)[None],
        collect(back_vgrad)[None],
        gate_grad[None],
        sink_grad,
    )


def solution(mesh):
    placed = (
        P("dp", "head", None),
        P("dp", "head", None, None),
        P("dp", "head", None, None),
        P("dp", "head", None, None),
        P("dp", "head", None),
        P("head"),
        P("dp", "head", None, None),
    )
    return jax.shard_map(
        per_device,
        mesh=mesh,
        in_specs=placed,
        out_specs=(
            P("dp", "head", None, None),
            P("dp", "head", None, None),
            P("dp", "head", None, None),
            P("dp", "head", None, None),
            P("dp", "head", None),
            P("head"),
        ),
        check_vma=False,
    )
```

profile of v0, /device:TPU:0, one launch (start us, length us, event | category | flops | bytes accessed | tf_op | source)
XLA Modules:
  0.0 204.0 jit_solution(5614113830701706993)
XLA Ops:
  2.3 7.6 %scatter_custom_fusion = bf16[2048]{0:T(1024)(128)(2,1)S(1)} fusion(s32[1024]{0:T(1024)S(1)} %bitcast.236, bf16[1024]{0:T(1024)(128)(2,1)S(1)} %broadcast.376, bf16[]{:T(256)} %constant.402.clone.1), kind=kCustom, calls=%fused_computation.130 | custom fusion | bytes 4098 | tf_op jit(solution)/shard_map/scatter | solution.py:208
  10.6 7.4 %all-to-all-start = ((bf16[16,4,32]{2,1,0:T(4,128)(2,1)}), bf16[16,4,32]{2,1,0:T(4,128)(2,1)S(1)}, u32[]{:S(2)}, u32[]{:S(2)}) async-start(bf16[16,4,32]{2,1,0:T(4,128)(2,1)} %reshape.293), calls=%async_computation | async-start | bytes 32768 | tf_op jit(solution)/shard_map/all_to_all | solution.py:216
  18.0 4.0 %scatter_custom_fusion.2 = bf16[2048,128]{1,0:T(8,128)(2,1)} fusion(s32[1024]{0:T(1024)S(1)} %bitcast.237, bf16[1,128,8,128]{3,2,1,0:T(8,128)(2,1)S(1)} %copy-done, bf16[]{:T(256)} %constant.402.clone.1), kind=kCustom, calls=%fused_computation.91 | custom fusion | bytes 786434 | tf_op jit(solution)/shard_map/scatter | solution.py:190
  22.0 2.5 %all-to-all-done = bf16[16,4,32]{2,1,0:T(4,128)(2,1)S(1)} async-done(((bf16[16,4,32]{2,1,0:T(4,128)(2,1)}), bf16[16,4,32]{2,1,0:T(4,128)(2,1)S(1)}, u32[]{:S(2)}, u32[]{:S(2)}) %all-to-all-start) | async-done | bytes 4128 | tf_op jit(solution)/shard_map/all_to_all | solution.py:216
  24.5 3.7 %all-to-all-start.2 = ((bf16[16,4,32,128]{3,2,1,0:T(8,128)(2,1)}), bf16[16,4,32,128]{3,2,1,0:T(8,128)(2,1)S(1)}, u32[]{:S(2)}, u32[]{:S(2)}) async-start(bf16[16,4,32,128]{3,2,1,0:T(8,128)(2,1)} %bitcast.7), calls=%async_computation.2 | async-start | bytes 1048576 | tf_op jit(solution)/shard_map/all_to_all | solution.py:214
  28.2 4.0 %scatter_custom_fusion.1 = bf16[2048,128]{1,0:T(8,128)(2,1)} fusion(s32[1024]{0:T(1024)S(1)} %bitcast.238, bf16[1,128,8,128]{3,2,1,0:T(8,128)(2,1)S(1)} %copy-done.18, bf16[]{:T(256)} %constant.402.clone.1), kind=kCustom, calls=%fused_computation.93 | custom fusion | bytes 786434 | tf_op jit(solution)/shard_map/scatter | solution.py:190
  32.2 10.2 %all-to-all-done.2 = bf16[16,4,32,128]{3,2,1,0:T(8,128)(2,1)S(1)} async-done(((bf16[16,4,32,128]{3,2,1,0:T(8,128)(2,1)}), bf16[16,4,32,128]{3,2,1,0:T(8,128)(2,1)S(1)}, u32[]{:S(2)}, u32[]{:S(2)}) %all-to-all-start.2) | async-done | bytes 524320 | tf_op jit(solution)/shard_map/all_to_all | solution.py:214
  42.4 4.3 %all-to-all-start.1 = ((bf16[16,4,32,128]{3,2,1,0:T(8,128)(2,1)}), bf16[16,4,32,128]{3,2,1,0:T(8,128)(2,1)S(1)}, u32[]{:S(2)}, u32[]{:S(2)}) async-start(bf16[16,4,32,128]{3,2,1,0:T(8,128)(2,1)} %bitcast.4), calls=%async_computation.1 | async-start | bytes 1048576 | tf_op jit(solution)/shard_map/all_to_all | solution.py:213
  47.6 4.5 %scatter_custom_fusion.4 = bf16[2048,128]{1,0:T(8,128)(2,1)} fusion(s32[1024]{0:T(1024)S(1)} %bitcast.239, bf16[1,128,8,128]{3,2,1,0:T(8,128)(2,1)S(1)} %copy-done.4, f32[1024]{0:T(1024)S(1)} %exponential_divide_fusion, bf16[]{:T(256)} %constant.402.clone.1), kind=kCustom, calls=%fused_computation.88 | custom fusion | flops 393216 | bytes 790530 | tf_op jit(solution)/shard_map/scatter | solution.py:190
  52.1 8.8 %all-to-all-done.1 = bf16[16,4,32,128]{3,2,1,0:T(8,128)(2,1)S(1)} async-done(((bf16[16,4,32,128]{3,2,1,0:T(8,128)(2,1)}), bf16[16,4,32,128]{3,2,1,0:T(8,128)(2,1)S(1)}, u32[]{:S(2)}, u32[]{:S(2)}) %all-to-all-start.1) | async-done | bytes 524320 | tf_op jit(solution)/shard_map/all_to_all | solution.py:213
  61.0 4.3 %all-to-all-start.5 = ((bf16[16,4,32,128]{3,2,1,0:T(8,128)(2,1)}), bf16[16,4,32,128]{3,2,1,0:T(8,128)(2,1)S(1)}, u32[]{:S(2)}, u32[]{:S(2)}) async-start(bf16[16,4,32,128]{3,2,1,0:T(8,128)(2,1)} %bitcast.36), calls=%async_computation.5 | async-start | bytes 1048576 | tf_op jit(solution)/shard_map/all_to_all | solution.py:247
  65.3 4.0 %scatter_custom_fusion.3 = bf16[2048,128]{1,0:T(8,128)(2,1)} fusion(s32[1024]{0:T(1024)S(1)} %bitcast.240, bf16[1,128,8,128]{3,2,1,0:T(8,128)(2,1)S(1)} %copy-done.19, bf16[]{:T(256)} %constant.402.clone.1), kind=kCustom, calls=%fused_computation.89 | custom fusion | bytes 786434 | tf_op jit(solution)/shard_map/scatter | solution.py:190
  72.3 7.3 %all-to-all-done.5 = bf16[16,4,32,128]{3,2,1,0:T(8,128)(2,1)S(1)} async-done(((bf16[16,4,32,128]{3,2,1,0:T(8,128)(2,1)}), bf16[16,4,32,128]{3,2,1,0:T(8,128)(2,1)S(1)}, u32[]{:S(2)}, u32[]{:S(2)}) %all-to-all-start.5) | async-done | bytes 524320 | tf_op jit(solution)/shard_map/all_to_all | solution.py:247
  79.5 4.2 %all-to-all-start.3 = ((bf16[16,4,32,128]{3,2,1,0:T(8,128)(2,1)}), bf16[16,4,32,128]{3,2,1,0:T(8,128)(2,1)S(1)}, u32[]{:S(2)}, u32[]{:S(2)}) async-start(bf16[16,4,32,128]{3,2,1,0:T(8,128)(2,1)} %bitcast.11), calls=%async_computation.3 | async-start | bytes 1048576 | tf_op jit(solution)/shard_map/all_to_all | solution.py:215
  86.2 11.8 %all-to-all-done.3 = bf16[16,4,32,128]{3,2,1,0:T(8,128)(2,1)S(1)} async-done(((bf16[16,4,32,128]{3,2,1,0:T(8,128)(2,1)}), bf16[16,4,32,128]{3,2,1,0:T(8,128)(2,1)S(1)}, u32[]{:S(2)}, u32[]{:S(2)}) %all-to-all-start.3) | async-done | bytes 524320 | tf_op jit(solution)/shard_map/all_to_all | solution.py:215
  104.5 1.3 fusion.7
  114.4 4.2 %all-to-all-start.8 = ((bf16[16,4,32,128]{3,2,1,0:T(8,128)(2,1)}), bf16[16,4,32,128]{3,2,1,0:T(8,128)(2,1)S(1)}, u32[]{:S(2)}, u32[]{:S(2)}) async-start(bf16[16,4,32,128]{3,2,1,0:T(8,128)(2,1)} %pad_maximum_fusion.3), calls=%async_computation.8 | async-start | bytes 1048576 | tf_op jit(solution)/shard_map/all_to_all | solution.py:274
  121.0 1.6 fusion.6
  124.7 8.2 %all-to-all-done.8 = bf16[16,4,32,128]{3,2,1,0:T(8,128)(2,1)S(1)} async-done(((bf16[16,4,32,128]{3,2,1,0:T(8,128)(2,1)}), bf16[16,4,32,128]{3,2,1,0:T(8,128)(2,1)S(1)}, u32[]{:S(2)}, u32[]{:S(2)}) %all-to-all-start.8) | async-done | bytes 524320 | tf_op jit(solution)/shard_map/all_to_all | solution.py:274
  132.9 4.2 %all-to-all-start.7 = ((bf16[16,4,32,128]{3,2,1,0:T(8,128)(2,1)}), bf16[16,4,32,128]{3,2,1,0:T(8,128)(2,1)S(1)}, u32[]{:S(2)}, u32[]{:S(2)}) async-start(bf16[16,4,32,128]{3,2,1,0:T(8,128)(2,1)} %pad_maximum_fusion.2), calls=%async_computation.7 | async-start | bytes 1048576 | tf_op jit(solution)/shard_map/all_to_all | solution.py:271
  138.0 13.4 %all-to-all-done.7 = bf16[16,4,32,128]{3,2,1,0:T(8,128)(2,1)S(1)} async-done(((bf16[16,4,32,128]{3,2,1,0:T(8,128)(2,1)}), bf16[16,4,32,128]{3,2,1,0:T(8,128)(2,1)S(1)}, u32[]{:S(2)}, u32[]{:S(2)}) %all-to-all-start.7) | async-done | bytes 524320 | tf_op jit(solution)/shard_map/all_to_all | solution.py:271
  151.3 4.2 %all-to-all-start.4 = ((bf16[16,4,32,128]{3,2,1,0:T(8,128)(2,1)}), bf16[16,4,32,128]{3,2,1,0:T(8,128)(2,1)S(1)}, u32[]{:S(2)}, u32[]{:S(2)}) async-start(bf16[16,4,32,128]{3,2,1,0:T(8,128)(2,1)} %pad_maximum_fusion), calls=%async_computation.4 | async-start | bytes 1048576 | tf_op jit(solution)/shard_map/all_to_all | solution.py:244
  155.5 1.3 fusion.11
  161.1 8.6 %all-to-all-done.4 = bf16[16,4,32,128]{3,2,1,0:T(8,128)(2,1)S(1)} async-done(((bf16[16,4,32,128]{3,2,1,0:T(8,128)(2,1)}), bf16[16,4,32,128]{3,2,1,0:T(8,128)(2,1)S(1)}, u32[]{:S(2)}, u32[]{:S(2)}) %all-to-all-start.4) | async-done | bytes 524320 | tf_op jit(solution)/shard_map/all_to_all | solution.py:244
  169.8 4.2 %all-to-all-start.6 = ((bf16[16,4,32,128]{3,2,1,0:T(8,128)(2,1)}), bf16[16,4,32,128]{3,2,1,0:T(8,128)(2,1)S(1)}, u32[]{:S(2)}, u32[]{:S(2)}) async-start(bf16[16,4,32,128]{3,2,1,0:T(8,128)(2,1)} %pad_maximum_fusion.1), calls=%async_computation.6 | async-start | bytes 1048576 | tf_op jit(solution)/shard_map/all_to_all | solution.py:268
  173.9 1.3 multiply_reduce_fusion.8
  176.5 1.3 multiply_reduce_fusion.6
  180.4 5.4 %psum.7 = f32[4]{0:T(128)} all-reduce(f32[4]{0:T(128)S(1)} %pad_maximum_fusion.4), channel_id=1, replica_groups=mesh['dp'=2,'head'=16] {'dp'}, use_global_device_ids=true, to_apply=%region_28.29 | all-reduce | flops 4 | bytes 32 | tf_op jit(solution)/shard_map/psum | solution.py:278
  185.8 4.3 %gather_fusion.3 = bf16[1024,128]{1,0:T(8,128)(2,1)} fusion(bf16[2048,128]{1,0:T(8,128)(2,1)S(1)} %bitcast.179, s32[1024]{0:T(1024)S(1)} %broadcast_clamp_fusion), kind=kCustom, calls=%fused_computation.3 | custom fusion | bytes 528384 | tf_op jit(solution)/shard_map/gather | solution.py:195
  190.1 4.3 %gather_fusion.2 = bf16[1024,128]{1,0:T(8,128)(2,1)} fusion(bf16[2048,128]{1,0:T(8,128)(2,1)S(1)} %bitcast.180, s32[1024]{0:T(1024)S(1)} %broadcast_clamp_fusion), kind=kCustom, calls=%fused_computation.2 | custom fusion | bytes 528384 | tf_op jit(solution)/shard_map/gather | solution.py:195
  194.4 3.2 %gather_fusion = bf16[1024,128]{1,0:T(8,128)(2,1)S(1)} fusion(bf16[2048,128]{1,0:T(8,128)(2,1)S(1)} %bitcast.181, s32[1024]{0:T(1024)S(1)} %broadcast_clamp_fusion), kind=kCustom, calls=%fused_computation | custom fusion | bytes 528384 | tf_op jit(solution)/shard_map/gather | solution.py:195
  198.1 4.3 %gather_fusion.1 = bf16[1024,128]{1,0:T(8,128)(2,1)} fusion(bf16[2048,128]{1,0:T(8,128)(2,1)S(1)} %bitcast.182, s32[1024]{0:T(1024)S(1)} %broadcast_clamp_fusion), kind=kCustom, calls=%fused_computation.1 | custom fusion | bytes 528384 | tf_op jit(solution)/shard_map/gather | solution.py:195
  (142 shorter events, 36.7 us)
Async XLA Ops:
  0.6 17.3 %copy-start = (bf16[1,128,8,128]{3,2,1,0:T(8,128)(2,1)S(1)}, bf16[1,128,8,128]{3,2,1,0:T(8,128)(2,1)}, u32[]{:S(2)}) copy-start(bf16[1,128,8,128]{3,2,1,0:T(8,128)(2,1)} %param.9) | copy-start | bytes 786436
  10.6 13.9 %all-to-all-start = ((bf16[16,4,32]{2,1,0:T(4,128)(2,1)}), bf16[16,4,32]{2,1,0:T(4,128)(2,1)S(1)}, u32[]{:S(2)}, u32[]{:S(2)}) async-start(bf16[16,4,32]{2,1,0:T(4,128)(2,1)} %reshape.293), calls=%async_computation | async-start | bytes 32768 | tf_op jit(solution)/shard_map/all_to_all | solution.py:216
  24.5 3.7 %copy-start.18 = (bf16[1,128,8,128]{3,2,1,0:T(8,128)(2,1)S(1)}, bf16[1,128,8,128]{3,2,1,0:T(8,128)(2,1)}, u32[]{:S(2)}) copy-start(bf16[1,128,8,128]{3,2,1,0:T(8,128)(2,1)} %param.8) | copy-start | bytes 786436
  24.5 17.9 %all-to-all-start.2 = ((bf16[16,4,32,128]{3,2,1,0:T(8,128)(2,1)}), bf16[16,4,32,128]{3,2,1,0:T(8,128)(2,1)S(1)}, u32[]{:S(2)}, u32[]{:S(2)}) async-start(bf16[16,4,32,128]{3,2,1,0:T(8,128)(2,1)} %bitcast.7), calls=%async_computation.2 | async-start | bytes 1048576 | tf_op jit(solution)/shard_map/all_to_all | solution.py:214
  42.4 4.3 %copy-start.28 = (f32[1,128,8]{1,2,0:T(8,128)S(1)}, f32[1,128,8]{1,2,0:T(8,128)}, u32[]{:S(2)}) copy-start(f32[1,128,8]{1,2,0:T(8,128)} %param.11) | copy-start | bytes 12292
  42.4 18.5 %all-to-all-start.1 = ((bf16[16,4,32,128]{3,2,1,0:T(8,128)(2,1)}), bf16[16,4,32,128]{3,2,1,0:T(8,128)(2,1)S(1)}, u32[]{:S(2)}, u32[]{:S(2)}) async-start(bf16[16,4,32,128]{3,2,1,0:T(8,128)(2,1)} %bitcast.4), calls=%async_computation.1 | async-start | bytes 1048576 | tf_op jit(solution)/shard_map/all_to_all | solution.py:213
  61.0 4.3 %copy-start.19 = (bf16[1,128,8,128]{3,2,1,0:T(8,128)(2,1)S(1)}, bf16[1,128,8,128]{3,2,1,0:T(8,128)(2,1)}, u32[]{:S(2)}) copy-start(bf16[1,128,8,128]{3,2,1,0:T(8,128)(2,1)} %param.10) | copy-start | bytes 786436
  61.0 18.6 %all-to-all-start.5 = ((bf16[16,4,32,128]{3,2,1,0:T(8,128)(2,1)}), bf16[16,4,32,128]{3,2,1,0:T(8,128)(2,1)S(1)}, u32[]{:S(2)}, u32[]{:S(2)}) async-start(bf16[16,4,32,128]{3,2,1,0:T(8,128)(2,1)} %bitcast.36), calls=%async_computation.5 | async-start | bytes 1048576 | tf_op jit(solution)/shard_map/all_to_all | solution.py:247
  65.3 4.0 %copy-start.30 = (f32[4]{0:T(128)S(1)}, f32[4]{0:T(128)}, u32[]{:S(2)}) copy-start(f32[4]{0:T(128)} %param.12) | copy-start | bytes 52
  71.1 30.0 %copy-start.10 = (bf16[16,1,32,128]{3,2,1,0:T(8,128)(2,1)}, bf16[16,1,32,128]{3,2,1,0:T(8,128)(2,1)S(1)}, u32[]{:S(2)}) copy-start(bf16[16,1,32,128]{3,2,1,0:T(8,128)(2,1)S(1)} %get-tuple-element.1312) | copy-start | bytes 393220
  71.1 35.6 %copy-start.8 = (bf16[16,1,32,128]{3,2,1,0:T(8,128)(2,1)}, bf16[16,1,32,128]{3,2,1,0:T(8,128)(2,1)S(1)}, u32[]{:S(2)}) copy-start(bf16[16,1,32,128]{3,2,1,0:T(8,128)(2,1)S(1)} %get-tuple-element.1314) | copy-start | bytes 393220
  71.9 34.8 %copy-start.15 = (bf16[16,1,32,128]{3,2,1,0:T(8,128)(2,1)}, bf16[16,1,32,128]{3,2,1,0:T(8,128)(2,1)S(1)}, u32[]{:S(2)}) copy-start(bf16[16,1,32,128]{3,2,1,0:T(8,128)(2,1)S(1)} %get-tuple-element.1318) | copy-start | bytes 393220
  79.5 18.4 %all-to-all-start.3 = ((bf16[16,4,32,128]{3,2,1,0:T(8,128)(2,1)}), bf16[16,4,32,128]{3,2,1,0:T(8,128)(2,1)S(1)}, u32[]{:S(2)}, u32[]{:S(2)}) async-start(bf16[16,4,32,128]{3,2,1,0:T(8,128)(2,1)} %bitcast.11), calls=%async_computation.3 | async-start | bytes 1048576 | tf_op jit(solution)/shard_map/all_to_all | solution.py:215
  85.9 17.6 %copy-start.26 = (bf16[16,1,32,128]{3,2,1,0:T(8,128)(2,1)}, bf16[16,1,32,128]{3,2,1,0:T(8,128)(2,1)S(1)}, u32[]{:S(2)}) copy-start(bf16[16,1,32,128]{3,2,1,0:T(8,128)(2,1)S(1)} %get-tuple-element.1308) | copy-start | bytes 393220
  111.5 8.4 %copy-start.3 = (f32[512,512]{0,1:T(8,128)}, f32[512,512]{0,1:T(8,128)S(1)}, u32[]{:S(2)}) copy-start(f32[512,512]{0,1:T(8,128)S(1)} %get-tuple-element.1333) | copy-start | bytes 3145732
  114.4 18.4 %all-to-all-start.8 = ((bf16[16,4,32,128]{3,2,1,0:T(8,128)(2,1)}), bf16[16,4,32,128]{3,2,1,0:T(8,128)(2,1)S(1)}, u32[]{:S(2)}, u32[]{:S(2)}) async-start(bf16[16,4,32,128]{3,2,1,0:T(8,128)(2,1)} %pad_maximum_fusion.3), calls=%async_computation.8 | async-start | bytes 1048576 | tf_op jit(solution)/shard_map/all_to_all | solution.py:274
  118.6 1.3 copy-start.22
  118.6 1.3 copy-start.24
  121.0 1.6 copy-start.14
  122.6 2.0 %copy-start.1 = (bf16[512,512]{0,1:T(8,128)(2,1)}, bf16[512,512]{0,1:T(8,128)(2,1)S(1)}, u32[]{:S(2)}) copy-start(bf16[512,512]{0,1:T(8,128)(2,1)S(1)} %fusion.6) | copy-start | bytes 1572868
  122.7 1.0 copy-start.16
  122.7 1.1 copy-start.17
  124.7 12.4 %copy-start.20 = (bf16[512,128]{1,0:T(8,128)(2,1)S(1)}, bf16[512,128]{1,0:T(8,128)(2,1)}, u32[]{:S(2)}) copy-start(bf16[512,128]{1,0:T(8,128)(2,1)} %get-tuple-element.1337) | copy-start | bytes 393220
  124.7 12.4 %copy-start.23 = (bf16[512,128]{1,0:T(8,128)(2,1)S(1)}, bf16[512,128]{1,0:T(8,128)(2,1)}, u32[]{:S(2)}) copy-start(bf16[512,128]{1,0:T(8,128)(2,1)} %get-tuple-element.1343) | copy-start | bytes 393220
  124.7 12.4 %copy-start.25 = (bf16[512,128]{1,0:T(8,128)(2,1)S(1)}, bf16[512,128]{1,0:T(8,128)(2,1)}, u32[]{:S(2)}) copy-start(bf16[512,128]{1,0:T(8,128)(2,1)} %get-tuple-element.1339) | copy-start | bytes 393220
  124.7 12.4 %copy-start.27 = (bf16[512,128]{1,0:T(8,128)(2,1)S(1)}, bf16[512,128]{1,0:T(8,128)(2,1)}, u32[]{:S(2)}) copy-start(bf16[512,128]{1,0:T(8,128)(2,1)} %get-tuple-element.1341) | copy-start | bytes 393220
  132.9 18.4 %all-to-all-start.7 = ((bf16[16,4,32,128]{3,2,1,0:T(8,128)(2,1)}), bf16[16,4,32,128]{3,2,1,0:T(8,128)(2,1)S(1)}, u32[]{:S(2)}, u32[]{:S(2)}) async-start(bf16[16,4,32,128]{3,2,1,0:T(8,128)(2,1)} %pad_maximum_fusion.2), calls=%async_computation.7 | async-start | bytes 1048576 | tf_op jit(solution)/shard_map/all_to_all | solution.py:271
  151.3 18.4 %all-to-all-start.4 = ((bf16[16,4,32,128]{3,2,1,0:T(8,128)(2,1)}), bf16[16,4,32,128]{3,2,1,0:T(8,128)(2,1)S(1)}, u32[]{:S(2)}, u32[]{:S(2)}) async-start(bf16[16,4,32,128]{3,2,1,0:T(8,128)(2,1)} %pad_maximum_fusion), calls=%async_computation.4 | async-start | bytes 1048576 | tf_op jit(solution)/shard_map/all_to_all | solution.py:244
  155.5 2.5 %copy-start.11 = (bf16[16,1,32,128]{3,2,1,0:T(8,128)(2,1)S(1)}, bf16[16,1,32,128]{3,2,1,0:T(8,128)(2,1)}, u32[]{:S(2)}) copy-start(bf16[16,1,32,128]{3,2,1,0:T(8,128)(2,1)} %copy-done.10) | copy-start | bytes 393220
  158.9 1.1 copy-start.7
  169.8 28.4 %all-to-all-start.6 = ((bf16[16,4,32,128]{3,2,1,0:T(8,128)(2,1)}), bf16[16,4,32,128]{3,2,1,0:T(8,128)(2,1)S(1)}, u32[]{:S(2)}, u32[]{:S(2)}) async-start(bf16[16,4,32,128]{3,2,1,0:T(8,128)(2,1)} %pad_maximum_fusion.1), calls=%async_computation.6 | async-start | bytes 1048576 | tf_op jit(solution)/shard_map/all_to_all | solution.py:268
  194.4 3.2 %copy-start.5 = (bf16[1,128,8,128]{3,2,1,0:T(8,128)(2,1)S(1)}, bf16[1,128,8,128]{3,2,1,0:T(8,128)(2,1)}, u32[]{:S(2)}) copy-start(bf16[1,128,8,128]{3,2,1,0:T(8,128)(2,1)} %param.13) | copy-start | bytes 786436
  (8 other events, 7.3 us)
where the time goes:
time: 205 us; the launch traced here: 204 us
  waiting for transfers between devices  70.8 us (35%)
  local copies, waits for them, and re-layouts  44.4 us (22%)
  starting transfers between devices  40.5 us (20%)
  other arithmetic  22.6 us (11%)
  matrix products  16.5 us (8%)
  blocking collectives  5.42 us (3%)
  between operations  3.8 us (2%)
    gather x4, local copies, waits for them, and re-layouts, collect(): buffer.reshape(buffer_rows, buffer.shape[-1])[target]  16.1 us
    all_to_all x1, waiting for transfers between devices, per_device(): lax.all_to_all(jnp.stack(kgrad_list, axis=1), 'head', split_axis=0, conca...  13.4 us
    scatter x3, local copies, waits for them, and re-layouts, spread_out(): jnp.zeros((buffer_rows, flat_rows.shape[-1]), flat_rows.dtype).at[target]  12 us
    all_to_all x1, waiting for transfers between devices, per_device(): lax.all_to_all(send_value, 'head', split_axis=0, concat_axis=0, tiled=True)  11.8 us
    all_to_all x1, waiting for transfers between devices, per_device(): lax.all_to_all(send_key, 'head', split_axis=0, concat_axis=0, tiled=True)  10.2 us
    all_to_all x1, waiting for transfers between devices, per_device(): lax.all_to_all(send_query, 'head', split_axis=0, concat_axis=0, tiled=True)  8.84 us
    all_to_all x1, waiting for transfers between devices, per_device(): lax.all_to_all(jnp.stack(out_list, axis=1), 'head', split_axis=0, concat_...  8.62 us
    all_to_all x1, waiting for transfers between devices, per_device(): lax.all_to_all(jnp.stack(vgrad_list, axis=1), 'head', split_axis=0, conca...  8.16 us
  transfers between devices with their start and end apart: 9, of which 8 were waited for; matrix products, arithmetic and copies ran while one was open for 24% of the time, Pallas kernels for 0%

commit v1 on v0

--- a/solution.py
+++ b/solution.py
@@ -244,7 +244,26 @@
     back_out = lax.all_to_all(
         jnp.stack(out_list, axis=1), "head", split_axis=0, concat_axis=0, tiled=True
     )
-    recv_cot = lax.all_to_all(send_cot, "head", split_axis=0, concat_axis=0, tiled=True)
+    small = lax.axis_size("head")
+    newest = lax.axis_index("head")
+    parts_out, found_now = (small, newest)
+    local_part = send_cot.shape[0] // parts_out
+    w1 = list(send_cot.shape)
+    w1[0] = local_part
+    clean = w1[0]
+    w1[0] = clean * parts_out
+    recv_cot = jnp.zeros(w1, send_cot.dtype)
+    for no in range(parts_out):
+        upper = lax.dynamic_slice_in_dim(
+            send_cot, (found_now ^ no) * local_part, local_part, axis=0
+        )
+        if no:
+            upper = lax.ppermute(
+                upper, "head", perm=[(dev_i, dev_i ^ no) for dev_i in range(parts_out)]
+            )
+        recv_cot = lax.dynamic_update_slice_in_dim(
+            recv_cot, upper, (found_now ^ no) * clean, axis=0
+        )
     for head_slot in range(local_heads):
         pieces, live_use, gather_order, landing, used_blocks = prepared[head_slot]
         cot_rows = pick_rows(recv_cot, head_slot)

time: 205 us -> 243 us (1.19)
  waiting for transfers between devices: 70.8 us -> 93.3 us
  starting transfers between devices: 40.5 us -> 53.8 us
    ppermute x0 -> x15, waiting for transfers between devices: none -> 39.7 us  [per_device(): lax.ppermute(upper, 'head', perm=[(dev_i, dev_i ^ no) for dev_i in range(...]
    ppermute x0 -> x15, starting transfers between devices: none -> 15.9 us  [per_device(): lax.ppermute(upper, 'head', perm=[(dev_i, dev_i ^ no) for dev_i in range(...]
    all_to_all x1, waiting for transfers between devices: 10.2 us -> 0.01 us  [per_device(): lax.all_to_all(send_key, 'head', split_axis=0, concat_axis=0, tiled=True)]
    all_to_all x1 -> x0, waiting for transfers between devices: 7.28 us -> none  [per_device(): lax.all_to_all(send_cot, 'head', split_axis=0, concat_axis=0, tiled=True)]
    all_to_all x1 -> x0, starting transfers between devices: 4.3 us -> none  [per_device(): lax.all_to_all(send_cot, 'head', split_axis=0, concat_axis=0, tiled=True)]
    all_to_all x1, waiting for transfers between devices: 8.84 us -> 12.8 us  [per_device(): lax.all_to_all(send_query, 'head', split_axis=0, concat_axis=0, tiled=True)]
    all_to_all x1, waiting for transfers between devices: 2.51 us -> 0.01 us  [per_device(): lax.all_to_all(filled, 'head', split_axis=0, concat_axis=0, tiled=True)]
  transfers between devices with their start and end apart: 9 -> 23, of which waited for: 8 -> 15; matrix products, arithmetic and copies ran while one was open for 24% -> 20% of each run, Pallas kernels for 0% -> 0%
where the time goes in v1:
time: 243 us; the launch traced here: 241 us
  waiting for transfers between devices  93.3 us (38%)
  starting transfers between devices  53.8 us (22%)
  local copies, waits for them, and re-layouts  46.4 us (19%)
  other arithmetic  22 us (9%)
  matrix products  16.3 us (7%)
  blocking collectives  5.42 us (2%)
  between operations  4.01 us (2%)
    ppermute x15, waiting for transfers between devices, per_device(): lax.ppermute(upper, 'head', perm=[(dev_i, dev_i ^ no) for dev_i in range(...  39.7 us
    gather x4, local copies, waits for them, and re-layouts, collect(): buffer.reshape(buffer_rows, buffer.shape[-1])[target]  16.1 us
    ppermute x15, starting transfers between devices, per_device(): lax.ppermute(upper, 'head', perm=[(dev_i, dev_i ^ no) for dev_i in range(...  15.9 us
    all_to_all x1, waiting for transfers between devices, per_device(): lax.all_to_all(jnp.stack(kgrad_list, axis=1), 'head', split_axis=0, conca...  13.4 us
    all_to_all x1, waiting for transfers between devices, per_device(): lax.all_to_all(send_query, 'head', split_axis=0, concat_axis=0, tiled=True)  12.8 us
    scatter x3, local copies, waits for them, and re-layouts, spread_out(): jnp.zeros((buffer_rows, flat_rows.shape[-1]), flat_rows.dtype).at[target]  12 us
    all_to_all x1, waiting for transfers between devices, per_device(): lax.all_to_all(send_value, 'head', split_axis=0, concat_axis=0, tiled=True)  10.8 us
    all_to_all x1, waiting for transfers between devices, per_device(): lax.all_to_all(jnp.stack(out_list, axis=1), 'head', split_axis=0, concat_...  8.63 us
  transfers between devices with their start and end apart: 23, of which 15 were waited for; matrix products, arithmetic and copies ran while one was open for 20% of the time, Pallas kernels for 0%

profile of v1, /device:TPU:0, one launch (start us, length us, event | category | flops | bytes accessed | tf_op | source)
XLA Modules:
  0.0 241.3 jit_solution(17973165538887102105)
XLA Ops:
  2.3 7.6 %scatter_custom_fusion = bf16[2048]{0:T(1024)(128)(2,1)S(1)} fusion(s32[1024]{0:T(1024)S(1)} %bitcast.270, bf16[1024]{0:T(1024)(128)(2,1)S(1)} %broadcast.376, bf16[]{:T(256)} %constant.422.clone.1), kind=kCustom, calls=%fused_computation.161 | custom fusion | bytes 4098 | tf_op jit(solution)/shard_map/scatter | solution.py:208
  10.6 7.4 %all-to-all-start = ((bf16[16,4,32]{2,1,0:T(4,128)(2,1)}), bf16[16,4,32]{2,1,0:T(4,128)(2,1)S(1)}, u32[]{:S(2)}, u32[]{:S(2)}) async-start(bf16[16,4,32]{2,1,0:T(4,128)(2,1)} %reshape.293), calls=%async_computation | async-start | bytes 32768 | tf_op jit(solution)/shard_map/all_to_all | solution.py:216
  19.7 3.8 %scatter_custom_fusion.4 = bf16[2048,128]{1,0:T(8,128)(2,1)S(1)} fusion(s32[1024]{0:T(1024)S(1)} %bitcast.271, bf16[1,128,8,128]{3,2,1,0:T(8,128)(2,1)S(1)} %copy-done.4, f32[1024]{0:T(1024)S(1)} %exponential_divide_fusion, bf16[]{:T(256)} %constant.422.clone.1), kind=kCustom, calls=%fused_computation.88 | custom fusion | flops 393216 | bytes 790530 | tf_op jit(solution)/shard_map/scatter | solution.py:190
  23.7 4.4 %collective-permute-start.14 = (bf16[1,4,32,128]{3,2,1,0:T(8,128)(2,1)S(1)}, bf16[1,4,32,128]{3,2,1,0:T(8,128)(2,1)S(1)}, u32[]{:S(2)}, u32[]{:S(2)}) collective-permute-start(bf16[1,4,32,128]{3,2,1,0:T(8,128)(2,1)S(1)} %get-tuple-element.1312), channel_id=1, source_target_pairs={{0,15},{1,14},{2,13},{3,12},{4,11},{5,10},{6,9},{7,8},{8,7},{9,6},... | collective-permute-start | bytes 98312 | tf_op jit(solution)/shard_map/ppermute | solution.py:261
  33.5 4.0 %scatter_custom_fusion.3 = bf16[2048,128]{1,0:T(8,128)(2,1)} fusion(s32[1024]{0:T(1024)S(1)} %bitcast.272, bf16[1,128,8,128]{3,2,1,0:T(8,128)(2,1)S(1)} %copy-done, bf16[]{:T(256)} %constant.422.clone.1), kind=kCustom, calls=%fused_computation.89 | custom fusion | bytes 786434 | tf_op jit(solution)/shard_map/scatter | solution.py:190
  37.4 4.0 %scatter_custom_fusion.2 = bf16[2048,128]{1,0:T(8,128)(2,1)} fusion(s32[1024]{0:T(1024)S(1)} %bitcast.273, bf16[1,128,8,128]{3,2,1,0:T(8,128)(2,1)S(1)} %copy-done.18, bf16[]{:T(256)} %constant.422.clone.1), kind=kCustom, calls=%fused_computation.91 | custom fusion | bytes 786434 | tf_op jit(solution)/shard_map/scatter | solution.py:190
  41.4 4.0 %scatter_custom_fusion.1 = bf16[2048,128]{1,0:T(8,128)(2,1)} fusion(s32[1024]{0:T(1024)S(1)} %bitcast.274, bf16[1,128,8,128]{3,2,1,0:T(8,128)(2,1)S(1)} %copy-done.19, bf16[]{:T(256)} %constant.422.clone.1), kind=kCustom, calls=%fused_computation.93 | custom fusion | bytes 786434 | tf_op jit(solution)/shard_map/scatter | solution.py:190
  45.4 5.7 %all-to-all-start.2 = ((bf16[16,4,32,128]{3,2,1,0:T(8,128)(2,1)}), bf16[16,4,32,128]{3,2,1,0:T(8,128)(2,1)S(1)}, u32[]{:S(2)}, u32[]{:S(2)}) async-start(bf16[16,4,32,128]{3,2,1,0:T(8,128)(2,1)} %bitcast.7), calls=%async_computation.2 | async-start | bytes 1048576 | tf_op jit(solution)/shard_map/all_to_all | solution.py:214
  53.6 4.3 %collective-permute-done.1 = bf16[1,4,32,128]{3,2,1,0:T(8,128)(2,1)S(1)} collective-permute-done((bf16[1,4,32,128]{3,2,1,0:T(8,128)(2,1)S(1)}, bf16[1,4,32,128]{3,2,1,0:T(8,128)(2,1)S(1)}, u32[]{:S(2)}, u32[]{:S(2)}) %collective-permute-start.1) | collective-permute-done | bytes 32800 | tf_op jit(solution)/shard_map/ppermute | solution.py:261
  57.9 3.6 %collective-permute-done.2 = bf16[1,4,32,128]{3,2,1,0:T(8,128)(2,1)S(1)} collective-permute-done((bf16[1,4,32,128]{3,2,1,0:T(8,128)(2,1)S(1)}, bf16[1,4,32,128]{3,2,1,0:T(8,128)(2,1)S(1)}, u32[]{:S(2)}, u32[]{:S(2)}) %collective-permute-start.2) | collective-permute-done | bytes 32800 | tf_op jit(solution)/shard_map/ppermute | solution.py:261
  61.5 4.2 %collective-permute-done.3 = bf16[1,4,32,128]{3,2,1,0:T(8,128)(2,1)S(1)} collective-permute-done((bf16[1,4,32,128]{3,2,1,0:T(8,128)(2,1)S(1)}, bf16[1,4,32,128]{3,2,1,0:T(8,128)(2,1)S(1)}, u32[]{:S(2)}, u32[]{:S(2)}) %collective-permute-start.3) | collective-permute-done | bytes 32800 | tf_op jit(solution)/shard_map/ppermute | solution.py:261
  65.7 3.3 %collective-permute-done.4 = bf16[1,4,32,128]{3,2,1,0:T(8,128)(2,1)S(1)} collective-permute-done((bf16[1,4,32,128]{3,2,1,0:T(8,128)(2,1)S(1)}, bf16[1,4,32,128]{3,2,1,0:T(8,128)(2,1)S(1)}, u32[]{:S(2)}, u32[]{:S(2)}) %collective-permute-start.4) | collective-permute-done | bytes 32800 | tf_op jit(solution)/shard_map/ppermute | solution.py:261
  69.8 4.0 %collective-permute-done.5 = bf16[1,4,32,128]{3,2,1,0:T(8,128)(2,1)S(1)} collective-permute-done((bf16[1,4,32,128]{3,2,1,0:T(8,128)(2,1)S(1)}, bf16[1,4,32,128]{3,2,1,0:T(8,128)(2,1)S(1)}, u32[]{:S(2)}, u32[]{:S(2)}) %collective-permute-start.5) | collective-permute-done | bytes 32800 | tf_op jit(solution)/shard_map/ppermute | solution.py:261
  73.8 4.2 %collective-permute-done.6 = bf16[1,4,32,128]{3,2,1,0:T(8,128)(2,1)S(1)} collective-permute-done((bf16[1,4,32,128]{3,2,1,0:T(8,128)(2,1)S(1)}, bf16[1,4,32,128]{3,2,1,0:T(8,128)(2,1)S(1)}, u32[]{:S(2)}, u32[]{:S(2)}) %collective-permute-start.6) | collective-permute-done | bytes 32800 | tf_op jit(solution)/shard_map/ppermute | solution.py:261
  82.9 4.3 %collective-permute-done.8 = bf16[1,4,32,128]{3,2,1,0:T(8,128)(2,1)S(1)} collective-permute-done((bf16[1,4,32,128]{3,2,1,0:T(8,128)(2,1)S(1)}, bf16[1,4,32,128]{3,2,1,0:T(8,128)(2,1)S(1)}, u32[]{:S(2)}, u32[]{:S(2)}) %collective-permute-start.8) | collective-permute-done | bytes 32800 | tf_op jit(solution)/shard_map/ppermute | solution.py:261
  89.8 3.7 %collective-permute-done.9 = bf16[1,4,32,128]{3,2,1,0:T(8,128)(2,1)S(1)} collective-permute-done((bf16[1,4,32,128]{3,2,1,0:T(8,128)(2,1)S(1)}, bf16[1,4,32,128]{3,2,1,0:T(8,128)(2,1)S(1)}, u32[]{:S(2)}, u32[]{:S(2)}) %collective-permute-start.9) | collective-permute-done | bytes 32800 | tf_op jit(solution)/shard_map/ppermute | solution.py:261
  93.6 5.3 %collective-permute-done.10 = bf16[1,4,32,128]{3,2,1,0:T(8,128)(2,1)S(1)} collective-permute-done((bf16[1,4,32,128]{3,2,1,0:T(8,128)(2,1)S(1)}, bf16[1,4,32,128]{3,2,1,0:T(8,128)(2,1)S(1)}, u32[]{:S(2)}, u32[]{:S(2)}) %collective-permute-start.10) | collective-permute-done | bytes 32800 | tf_op jit(solution)/shard_map/ppermute | solution.py:261
  99.0 4.0 %all-to-all-start.1 = ((bf16[16,4,32,128]{3,2,1,0:T(8,128)(2,1)}), bf16[16,4,32,128]{3,2,1,0:T(8,128)(2,1)S(1)}, u32[]{:S(2)}, u32[]{:S(2)}) async-start(bf16[16,4,32,128]{3,2,1,0:T(8,128)(2,1)} %bitcast.4), calls=%async_computation.1 | async-start | bytes 1048576 | tf_op jit(solution)/shard_map/all_to_all | solution.py:213
  104.4 12.8 %all-to-all-done.1 = bf16[16,4,32,128]{3,2,1,0:T(8,128)(2,1)S(1)} async-done(((bf16[16,4,32,128]{3,2,1,0:T(8,128)(2,1)}), bf16[16,4,32,128]{3,2,1,0:T(8,128)(2,1)S(1)}, u32[]{:S(2)}, u32[]{:S(2)}) %all-to-all-start.1) | async-done | bytes 524320 | tf_op jit(solution)/shard_map/all_to_all | solution.py:213
  117.2 4.2 %all-to-all-start.3 = ((bf16[16,4,32,128]{3,2,1,0:T(8,128)(2,1)}), bf16[16,4,32,128]{3,2,1,0:T(8,128)(2,1)S(1)}, u32[]{:S(2)}, u32[]{:S(2)}) async-start(bf16[16,4,32,128]{3,2,1,0:T(8,128)(2,1)} %bitcast.11), calls=%async_computation.3 | async-start | bytes 1048576 | tf_op jit(solution)/shard_map/all_to_all | solution.py:215
  124.9 10.8 %all-to-all-done.3 = bf16[16,4,32,128]{3,2,1,0:T(8,128)(2,1)S(1)} async-done(((bf16[16,4,32,128]{3,2,1,0:T(8,128)(2,1)}), bf16[16,4,32,128]{3,2,1,0:T(8,128)(2,1)S(1)}, u32[]{:S(2)}, u32[]{:S(2)}) %all-to-all-start.3) | async-done | bytes 524320 | tf_op jit(solution)/shard_map/all_to_all | solution.py:215
  151.7 4.2 %all-to-all-start.7 = ((bf16[16,4,32,128]{3,2,1,0:T(8,128)(2,1)}), bf16[16,4,32,128]{3,2,1,0:T(8,128)(2,1)S(1)}, u32[]{:S(2)}, u32[]{:S(2)}) async-start(bf16[16,4,32,128]{3,2,1,0:T(8,128)(2,1)} %pad_maximum_fusion.3), calls=%async_computation.7 | async-start | bytes 1048576 | tf_op jit(solution)/shard_map/all_to_all | solution.py:293
  162.0 8.2 %all-to-all-done.7 = bf16[16,4,32,128]{3,2,1,0:T(8,128)(2,1)S(1)} async-done(((bf16[16,4,32,128]{3,2,1,0:T(8,128)(2,1)}), bf16[16,4,32,128]{3,2,1,0:T(8,128)(2,1)S(1)}, u32[]{:S(2)}, u32[]{:S(2)}) %all-to-all-start.7) | async-done | bytes 524320 | tf_op jit(solution)/shard_map/all_to_all | solution.py:293
  170.2 4.2 %all-to-all-start.6 = ((bf16[16,4,32,128]{3,2,1,0:T(8,128)(2,1)}), bf16[16,4,32,128]{3,2,1,0:T(8,128)(2,1)S(1)}, u32[]{:S(2)}, u32[]{:S(2)}) async-start(bf16[16,4,32,128]{3,2,1,0:T(8,128)(2,1)} %pad_maximum_fusion.2), calls=%async_computation.6 | async-start | bytes 1048576 | tf_op jit(solution)/shard_map/all_to_all | solution.py:290
  175.3 13.4 %all-to-all-done.6 = bf16[16,4,32,128]{3,2,1,0:T(8,128)(2,1)S(1)} async-done(((bf16[16,4,32,128]{3,2,1,0:T(8,128)(2,1)}), bf16[16,4,32,128]{3,2,1,0:T(8,128)(2,1)S(1)}, u32[]{:S(2)}, u32[]{:S(2)}) %all-to-all-start.6) | async-done | bytes 524320 | tf_op jit(solution)/shard_map/all_to_all | solution.py:290
  188.6 4.2 %all-to-all-start.4 = ((bf16[16,4,32,128]{3,2,1,0:T(8,128)(2,1)}), bf16[16,4,32,128]{3,2,1,0:T(8,128)(2,1)S(1)}, u32[]{:S(2)}, u32[]{:S(2)}) async-start(bf16[16,4,32,128]{3,2,1,0:T(8,128)(2,1)} %pad_maximum_fusion), calls=%async_computation.4 | async-start | bytes 1048576 | tf_op jit(solution)/shard_map/all_to_all | solution.py:244
  198.4 8.6 %all-to-all-done.4 = bf16[16,4,32,128]{3,2,1,0:T(8,128)(2,1)S(1)} async-done(((bf16[16,4,32,128]{3,2,1,0:T(8,128)(2,1)}), bf16[16,4,32,128]{3,2,1,0:T(8,128)(2,1)S(1)}, u32[]{:S(2)}, u32[]{:S(2)}) %all-to-all-start.4) | async-done | bytes 524320 | tf_op jit(solution)/shard_map/all_to_all | solution.py:244
  207.1 4.2 %all-to-all-start.5 = ((bf16[16,4,32,128]{3,2,1,0:T(8,128)(2,1)}), bf16[16,4,32,128]{3,2,1,0:T(8,128)(2,1)S(1)}, u32[]{:S(2)}, u32[]{:S(2)}) async-start(bf16[16,4,32,128]{3,2,1,0:T(8,128)(2,1)} %pad_maximum_fusion.1), calls=%async_computation.5 | async-start | bytes 1048576 | tf_op jit(solution)/shard_map/all_to_all | solution.py:287
  217.7 5.4 %psum.7 = f32[4]{0:T(128)} all-reduce(f32[4]{0:T(128)S(1)} %pad_maximum_fusion.4), channel_id=1, replica_groups=mesh['dp'=2,'head'=16] {'dp'}, use_global_device_ids=true, to_apply=%region_28.29 | all-reduce | flops 4 | bytes 32 | tf_op jit(solution)/shard_map/psum | solution.py:297
  223.1 4.3 %gather_fusion.3 = bf16[1024,128]{1,0:T(8,128)(2,1)} fusion(bf16[2048,128]{1,0:T(8,128)(2,1)S(1)} %bitcast.211, s32[1024]{0:T(1024)S(1)} %broadcast_clamp_fusion), kind=kCustom, calls=%fused_computation.3 | custom fusion | bytes 528384 | tf_op jit(solution)/shard_map/gather | solution.py:195
  227.4 4.3 %gather_fusion.2 = bf16[1024,128]{1,0:T(8,128)(2,1)} fusion(bf16[2048,128]{1,0:T(8,128)(2,1)S(1)} %bitcast.212, s32[1024]{0:T(1024)S(1)} %broadcast_clamp_fusion), kind=kCustom, calls=%fused_computation.2 | custom fusion | bytes 528384 | tf_op jit(solution)/shard_map/gather | solution.py:195
  235.5 4.3 %gather_fusion.1 = bf16[1024,128]{1,0:T(8,128)(2,1)} fusion(bf16[2048,128]{1,0:T(8,128)(2,1)S(1)} %bitcast.214, s32[1024]{0:T(1024)S(1)} %broadcast_clamp_fusion), kind=kCustom, calls=%fused_computation.1 | custom fusion | bytes 528384 | tf_op jit(solution)/shard_map/gather | solution.py:195
  (188 shorter events, 62.7 us)
Async XLA Ops:
  0.6 32.8 %copy-start = (bf16[1,128,8,128]{3,2,1,0:T(8,128)(2,1)S(1)}, bf16[1,128,8,128]{3,2,1,0:T(8,128)(2,1)}, u32[]{:S(2)}) copy-start(bf16[1,128,8,128]{3,2,1,0:T(8,128)(2,1)} %param.10) | copy-start | bytes 786436
  10.6 34.9 %all-to-all-start = ((bf16[16,4,32]{2,1,0:T(4,128)(2,1)}), bf16[16,4,32]{2,1,0:T(4,128)(2,1)S(1)}, u32[]{:S(2)}, u32[]{:S(2)}) async-start(bf16[16,4,32]{2,1,0:T(4,128)(2,1)} %reshape.293), calls=%async_computation | async-start | bytes 32768 | tf_op jit(solution)/shard_map/all_to_all | solution.py:216
  23.7 79.3 %collective-permute-start.14 = (bf16[1,4,32,128]{3,2,1,0:T(8,128)(2,1)S(1)}, bf16[1,4,32,128]{3,2,1,0:T(8,128)(2,1)S(1)}, u32[]{:S(2)}, u32[]{:S(2)}) collective-permute-start(bf16[1,4,32,128]{3,2,1,0:T(8,128)(2,1)S(1)} %get-tuple-element.1312), channel_id=1, source_target_pairs={{0,15},{1,14},{2,13},{3,12},{4,11},{5,10},{6,9},{7,8},{8,7},{9,6},... | collective-permute-start | bytes 98312 | tf_op jit(solution)/shard_map/ppermute | solution.py:261
  28.0 75.0 %collective-permute-start.13 = (bf16[1,4,32,128]{3,2,1,0:T(8,128)(2,1)S(1)}, bf16[1,4,32,128]{3,2,1,0:T(8,128)(2,1)S(1)}, u32[]{:S(2)}, u32[]{:S(2)}) collective-permute-start(bf16[1,4,32,128]{3,2,1,0:T(8,128)(2,1)S(1)} %get-tuple-element.1313), channel_id=1, source_target_pairs={{0,14},{1,15},{2,12},{3,13},{4,10},{5,11},{6,8},{7,9},{8,6},{9,7},... | collective-permute-start | bytes 98312 | tf_op jit(solution)/shard_map/ppermute | solution.py:261
  28.4 74.5 %collective-permute-start.12 = (bf16[1,4,32,128]{3,2,1,0:T(8,128)(2,1)S(1)}, bf16[1,4,32,128]{3,2,1,0:T(8,128)(2,1)S(1)}, u32[]{:S(2)}, u32[]{:S(2)}) collective-permute-start(bf16[1,4,32,128]{3,2,1,0:T(8,128)(2,1)S(1)} %get-tuple-element.1314), channel_id=1, source_target_pairs={{0,13},{1,12},{2,15},{3,14},{4,9},{5,8},{6,11},{7,10},{8,5},{9,4},... | collective-permute-start | bytes 98312 | tf_op jit(solution)/shard_map/ppermute | solution.py:261
  31.6 67.4 %collective-permute-start.11 = (bf16[1,4,32,128]{3,2,1,0:T(8,128)(2,1)S(1)}, bf16[1,4,32,128]{3,2,1,0:T(8,128)(2,1)S(1)}, u32[]{:S(2)}, u32[]{:S(2)}) collective-permute-start(bf16[1,4,32,128]{3,2,1,0:T(8,128)(2,1)S(1)} %get-tuple-element.1315), channel_id=1, source_target_pairs={{0,12},{1,13},{2,14},{3,15},{4,8},{5,9},{6,10},{7,11},{8,4},{9,5},... | collective-permute-start | bytes 98312 | tf_op jit(solution)/shard_map/ppermute | solution.py:261
  31.8 19.8 %collective-permute-start = (bf16[1,4,32,128]{3,2,1,0:T(8,128)(2,1)S(1)}, bf16[1,4,32,128]{3,2,1,0:T(8,128)(2,1)S(1)}, u32[]{:S(2)}, u32[]{:S(2)}) collective-permute-start(bf16[1,4,32,128]{3,2,1,0:T(8,128)(2,1)S(1)} %get-tuple-element.1326), channel_id=1, source_target_pairs={{0,1},{1,0},{2,3},{3,2},{4,5},{5,4},{6,7},{7,6},{8,9},{9,8},{10,11... | collective-permute-start | bytes 98312 | tf_op jit(solution)/shard_map/ppermute | solution.py:261
  45.4 53.5 %all-to-all-start.2 = ((bf16[16,4,32,128]{3,2,1,0:T(8,128)(2,1)}), bf16[16,4,32,128]{3,2,1,0:T(8,128)(2,1)S(1)}, u32[]{:S(2)}, u32[]{:S(2)}) async-start(bf16[16,4,32,128]{3,2,1,0:T(8,128)(2,1)} %bitcast.7), calls=%async_computation.2 | async-start | bytes 1048576 | tf_op jit(solution)/shard_map/all_to_all | solution.py:214
  51.6 6.2 %collective-permute-start.1 = (bf16[1,4,32,128]{3,2,1,0:T(8,128)(2,1)S(1)}, bf16[1,4,32,128]{3,2,1,0:T(8,128)(2,1)S(1)}, u32[]{:S(2)}, u32[]{:S(2)}) collective-permute-start(bf16[1,4,32,128]{3,2,1,0:T(8,128)(2,1)S(1)} %get-tuple-element.1325), channel_id=1, source_target_pairs={{0,2},{1,3},{2,0},{3,1},{4,6},{5,7},{6,4},{7,5},{8,10},{9,11},{10,... | collective-permute-start | bytes 98312 | tf_op jit(solution)/shard_map/ppermute | solution.py:261
  57.9 3.6 %collective-permute-start.2 = (bf16[1,4,32,128]{3,2,1,0:T(8,128)(2,1)S(1)}, bf16[1,4,32,128]{3,2,1,0:T(8,128)(2,1)S(1)}, u32[]{:S(2)}, u32[]{:S(2)}) collective-permute-start(bf16[1,4,32,128]{3,2,1,0:T(8,128)(2,1)S(1)} %get-tuple-element.1324), channel_id=1, source_target_pairs={{0,3},{1,2},{2,1},{3,0},{4,7},{5,6},{6,5},{7,4},{8,11},{9,10},{10,... | collective-permute-start | bytes 98312 | tf_op jit(solution)/shard_map/ppermute | solution.py:261
  61.5 4.2 %collective-permute-start.3 = (bf16[1,4,32,128]{3,2,1,0:T(8,128)(2,1)S(1)}, bf16[1,4,32,128]{3,2,1,0:T(8,128)(2,1)S(1)}, u32[]{:S(2)}, u32[]{:S(2)}) collective-permute-start(bf16[1,4,32,128]{3,2,1,0:T(8,128)(2,1)S(1)} %get-tuple-element.1323), channel_id=1, source_target_pairs={{0,4},{1,5},{2,6},{3,7},{4,0},{5,1},{6,2},{7,3},{8,12},{9,13},{10,... | collective-permute-start | bytes 98312 | tf_op jit(solution)/shard_map/ppermute | solution.py:261
  65.6 3.3 %collective-permute-start.4 = (bf16[1,4,32,128]{3,2,1,0:T(8,128)(2,1)S(1)}, bf16[1,4,32,128]{3,2,1,0:T(8,128)(2,1)S(1)}, u32[]{:S(2)}, u32[]{:S(2)}) collective-permute-start(bf16[1,4,32,128]{3,2,1,0:T(8,128)(2,1)S(1)} %get-tuple-element.1322), channel_id=1, source_target_pairs={{0,5},{1,4},{2,7},{3,6},{4,1},{5,0},{6,3},{7,2},{8,13},{9,12},{10,... | collective-permute-start | bytes 98312 | tf_op jit(solution)/shard_map/ppermute | solution.py:261
  69.0 4.8 %collective-permute-start.5 = (bf16[1,4,32,128]{3,2,1,0:T(8,128)(2,1)S(1)}, bf16[1,4,32,128]{3,2,1,0:T(8,128)(2,1)S(1)}, u32[]{:S(2)}, u32[]{:S(2)}) collective-permute-start(bf16[1,4,32,128]{3,2,1,0:T(8,128)(2,1)S(1)} %get-tuple-element.1321), channel_id=1, source_target_pairs={{0,6},{1,7},{2,4},{3,5},{4,2},{5,3},{6,0},{7,1},{8,14},{9,15},{10,... | collective-permute-start | bytes 98312 | tf_op jit(solution)/shard_map/ppermute | solution.py:261
  73.8 4.2 %collective-permute-start.6 = (bf16[1,4,32,128]{3,2,1,0:T(8,128)(2,1)S(1)}, bf16[1,4,32,128]{3,2,1,0:T(8,128)(2,1)S(1)}, u32[]{:S(2)}, u32[]{:S(2)}) collective-permute-start(bf16[1,4,32,128]{3,2,1,0:T(8,128)(2,1)S(1)} %get-tuple-element.1320), channel_id=1, source_target_pairs={{0,7},{1,6},{2,5},{3,4},{4,3},{5,2},{6,1},{7,0},{8,15},{9,14},{10,... | collective-permute-start | bytes 98312 | tf_op jit(solution)/shard_map/ppermute | solution.py:261
  78.0 4.8 %collective-permute-start.7 = (bf16[1,4,32,128]{3,2,1,0:T(8,128)(2,1)S(1)}, bf16[1,4,32,128]{3,2,1,0:T(8,128)(2,1)S(1)}, u32[]{:S(2)}, u32[]{:S(2)}) collective-permute-start(bf16[1,4,32,128]{3,2,1,0:T(8,128)(2,1)S(1)} %get-tuple-element.1319), channel_id=1, source_target_pairs={{0,8},{1,9},{2,10},{3,11},{4,12},{5,13},{6,14},{7,15},{8,0},{9,1},... | collective-permute-start | bytes 98312 | tf_op jit(solution)/shard_map/ppermute | solution.py:261
  82.9 4.3 %collective-permute-start.8 = (bf16[1,4,32,128]{3,2,1,0:T(8,128)(2,1)S(1)}, bf16[1,4,32,128]{3,2,1,0:T(8,128)(2,1)S(1)}, u32[]{:S(2)}, u32[]{:S(2)}) collective-permute-start(bf16[1,4,32,128]{3,2,1,0:T(8,128)(2,1)S(1)} %get-tuple-element.1318), channel_id=1, source_target_pairs={{0,9},{1,8},{2,11},{3,10},{4,13},{5,12},{6,15},{7,14},{8,1},{9,0},... | collective-permute-start | bytes 98312 | tf_op jit(solution)/shard_map/ppermute | solution.py:261
  87.2 6.4 %collective-permute-start.9 = (bf16[1,4,32,128]{3,2,1,0:T(8,128)(2,1)S(1)}, bf16[1,4,32,128]{3,2,1,0:T(8,128)(2,1)S(1)}, u32[]{:S(2)}, u32[]{:S(2)}) collective-permute-start(bf16[1,4,32,128]{3,2,1,0:T(8,128)(2,1)S(1)} %get-tuple-element.1317), channel_id=1, source_target_pairs={{0,10},{1,11},{2,8},{3,9},{4,14},{5,15},{6,12},{7,13},{8,2},{9,3},... | collective-permute-start | bytes 98312 | tf_op jit(solution)/shard_map/ppermute | solution.py:261
  93.6 5.4 %collective-permute-start.10 = (bf16[1,4,32,128]{3,2,1,0:T(8,128)(2,1)S(1)}, bf16[1,4,32,128]{3,2,1,0:T(8,128)(2,1)S(1)}, u32[]{:S(2)}, u32[]{:S(2)}) collective-permute-start(bf16[1,4,32,128]{3,2,1,0:T(8,128)(2,1)S(1)} %get-tuple-element.1316), channel_id=1, source_target_pairs={{0,11},{1,10},{2,9},{3,8},{4,15},{5,14},{6,13},{7,12},{8,3},{9,2},... | collective-permute-start | bytes 98312 | tf_op jit(solution)/shard_map/ppermute | solution.py:261
  99.0 18.2 %all-to-all-start.1 = ((bf16[16,4,32,128]{3,2,1,0:T(8,128)(2,1)}), bf16[16,4,32,128]{3,2,1,0:T(8,128)(2,1)S(1)}, u32[]{:S(2)}, u32[]{:S(2)}) async-start(bf16[16,4,32,128]{3,2,1,0:T(8,128)(2,1)} %bitcast.4), calls=%async_computation.1 | async-start | bytes 1048576 | tf_op jit(solution)/shard_map/all_to_all | solution.py:213
  104.4 17.7 %copy-start.12 = (bf16[16,1,32,128]{3,2,1,0:T(8,128)(2,1)}, bf16[16,1,32,128]{3,2,1,0:T(8,128)(2,1)S(1)}, u32[]{:S(2)}) copy-start(bf16[16,1,32,128]{3,2,1,0:T(8,128)(2,1)S(1)} %get-tuple-element.1328) | copy-start | bytes 393220
  104.4 34.3 %copy-start.10 = (bf16[16,1,32,128]{3,2,1,0:T(8,128)(2,1)}, bf16[16,1,32,128]{3,2,1,0:T(8,128)(2,1)S(1)}, u32[]{:S(2)}) copy-start(bf16[16,1,32,128]{3,2,1,0:T(8,128)(2,1)S(1)} %get-tuple-element.1327) | copy-start | bytes 393220
  104.4 39.0 %copy-start.8 = (bf16[16,1,32,128]{3,2,1,0:T(8,128)(2,1)}, bf16[16,1,32,128]{3,2,1,0:T(8,128)(2,1)S(1)}, u32[]{:S(2)}) copy-start(bf16[16,1,32,128]{3,2,1,0:T(8,128)(2,1)S(1)} %get-tuple-element.1329) | copy-start | bytes 393220
  117.2 18.4 %all-to-all-start.3 = ((bf16[16,4,32,128]{3,2,1,0:T(8,128)(2,1)}), bf16[16,4,32,128]{3,2,1,0:T(8,128)(2,1)S(1)}, u32[]{:S(2)}, u32[]{:S(2)}) async-start(bf16[16,4,32,128]{3,2,1,0:T(8,128)(2,1)} %bitcast.11), calls=%async_computation.3 | async-start | bytes 1048576 | tf_op jit(solution)/shard_map/all_to_all | solution.py:215
  122.1 21.4 %copy-start.15 = (bf16[16,1,32,128]{3,2,1,0:T(8,128)(2,1)}, bf16[16,1,32,128]{3,2,1,0:T(8,128)(2,1)S(1)}, u32[]{:S(2)}) copy-start(bf16[16,1,32,128]{3,2,1,0:T(8,128)(2,1)S(1)} %get-tuple-element.1333) | copy-start | bytes 393220
  151.7 18.4 %all-to-all-start.7 = ((bf16[16,4,32,128]{3,2,1,0:T(8,128)(2,1)}), bf16[16,4,32,128]{3,2,1,0:T(8,128)(2,1)S(1)}, u32[]{:S(2)}, u32[]{:S(2)}) async-start(bf16[16,4,32,128]{3,2,1,0:T(8,128)(2,1)} %pad_maximum_fusion.3), calls=%async_computation.7 | async-start | bytes 1048576 | tf_op jit(solution)/shard_map/all_to_all | solution.py:293
  162.0 12.4 %copy-start.22 = (bf16[512,128]{1,0:T(8,128)(2,1)S(1)}, bf16[512,128]{1,0:T(8,128)(2,1)}, u32[]{:S(2)}) copy-start(bf16[512,128]{1,0:T(8,128)(2,1)} %get-tuple-element.1352) | copy-start | bytes 393220
  162.0 12.4 %copy-start.23 = (bf16[512,128]{1,0:T(8,128)(2,1)S(1)}, bf16[512,128]{1,0:T(8,128)(2,1)}, u32[]{:S(2)}) copy-start(bf16[512,128]{1,0:T(8,128)(2,1)} %get-tuple-element.1358) | copy-start | bytes 393220
  162.0 12.4 %copy-start.26 = (bf16[512,128]{1,0:T(8,128)(2,1)S(1)}, bf16[512,128]{1,0:T(8,128)(2,1)}, u32[]{:S(2)}) copy-start(bf16[512,128]{1,0:T(8,128)(2,1)} %get-tuple-element.1354) | copy-start | bytes 393220
  162.0 12.4 %copy-start.27 = (bf16[512,128]{1,0:T(8,128)(2,1)S(1)}, bf16[512,128]{1,0:T(8,128)(2,1)}, u32[]{:S(2)}) copy-start(bf16[512,128]{1,0:T(8,128)(2,1)} %get-tuple-element.1356) | copy-start | bytes 393220
  170.2 18.4 %all-to-all-start.6 = ((bf16[16,4,32,128]{3,2,1,0:T(8,128)(2,1)}), bf16[16,4,32,128]{3,2,1,0:T(8,128)(2,1)S(1)}, u32[]{:S(2)}, u32[]{:S(2)}) async-start(bf16[16,4,32,128]{3,2,1,0:T(8,128)(2,1)} %pad_maximum_fusion.2), calls=%async_computation.6 | async-start | bytes 1048576 | tf_op jit(solution)/shard_map/all_to_all | solution.py:290
  188.6 18.4 %all-to-all-start.4 = ((bf16[16,4,32,128]{3,2,1,0:T(8,128)(2,1)}), bf16[16,4,32,128]{3,2,1,0:T(8,128)(2,1)S(1)}, u32[]{:S(2)}, u32[]{:S(2)}) async-start(bf16[16,4,32,128]{3,2,1,0:T(8,128)(2,1)} %pad_maximum_fusion), calls=%async_computation.4 | async-start | bytes 1048576 | tf_op jit(solution)/shard_map/all_to_all | solution.py:244
  207.1 28.4 %all-to-all-start.5 = ((bf16[16,4,32,128]{3,2,1,0:T(8,128)(2,1)}), bf16[16,4,32,128]{3,2,1,0:T(8,128)(2,1)S(1)}, u32[]{:S(2)}, u32[]{:S(2)}) async-start(bf16[16,4,32,128]{3,2,1,0:T(8,128)(2,1)} %pad_maximum_fusion.1), calls=%async_computation.5 | async-start | bytes 1048576 | tf_op jit(solution)/shard_map/all_to_all | solution.py:287
  (22 other events, 40.8 us)
